TPU v7x, 32 devices: a whole 2x2x4 slice. The times are simulated.
32 devices in a mesh: pulse: 4 (over z), tile: 8 (over y, x, core).
Axes of the slice: x: 2, y: 2, z: 4, core: 2. Of those that a mesh axis runs over, the one named last changes fastest.
Arguments:
- raw: bfloat16 [2, 128, 2048], P(None, ('pulse', 'tile')), may hold values from -6 to 6
- filt: bfloat16 [2, 1024, 2048], replicated, may hold values from -0.125 to 0.125
- range_off: int32 [128], P(('pulse', 'tile')), may hold values from 0 to 1024
- fine: int32 [128], P(('pulse', 'tile')), may hold values from 0 to 3
- dop: int32 [128], P(('pulse', 'tile')), may hold values from 0 to 511
- pulse_order: int32 [32, 4], P(('pulse', 'tile')), may hold values from 0 to 3, each once within a row
- band_idx: int32 [8, 128], P(None, ('pulse', 'tile')), may hold values from 0 to 1023
Outputs:
- image: bfloat16 [2, 512, 32768], P(None, 'pulse', 'tile')
Inputs may be any that keep to these rules, and one draw needn't show every extreme that they name: `pulse_order`: each row is a permutation of 0 .. 3.
All inputs are finite; a program needn't handle non-finite values.
Results may differ from a plain program's by a relative error of at most 0.0065.
Values may be sent and summed in bfloat16 or wider, within the bound.
A program may use at most 192 MiB of HBM per device.

v0:
```python
import functools

import jax
import jax.numpy as jnp
from jax import lax
from jax.experimental import pallas as pl
from jax.experimental.pallas import tpu as pltpu
from jax.sharding import PartitionSpec as P

F32 = jnp.float32
BF16 = jnp.bfloat16
MESH = pl.DeviceIdType.MESH
LANES = 128
DOP_SPLIT = 32
VMEM_LIMIT = 60 * 1024 * 1024


def gather_kernel(
    n_pulse, n_tile, off_ref, raw_ref, meta_ref, win_ref, all_meta_ref,
    z_send, z_recv, t_send, t_recv, p_send, p_recv,
):
    me_p = lax.axis_index("pulse")
    me_t = lax.axis_index("tile")
    half = n_tile // 2
    core = me_t % 2
    chip = me_t // 2
    partner = chip * 2 + (1 - core)
    p_dev = raw_ref.shape[0] // 2
    raw_len = raw_ref.shape[1]
    win = win_ref.shape[-1]

    def pulse_peer(d):
        return lax.rem(me_p + d, n_pulse)

    def tile_peer(d):
        return lax.rem(chip + d, half) * 2 + core

    barrier = pltpu.get_barrier_semaphore()
    for d in range(1, n_pulse):
        pl.semaphore_signal(barrier, 1, device_id=(pulse_peer(d), me_t), device_id_type=MESH)
    for d in range(1, half):
        pl.semaphore_signal(barrier, 1, device_id=(me_p, tile_peer(d)), device_id_type=MESH)
    pl.semaphore_signal(barrier, 1, device_id=(me_p, partner), device_id_type=MESH)

    raw = raw_ref[...].astype(F32)
    row = lax.broadcasted_iota(jnp.int32, (2 * p_dev, win), 0)
    cut = jnp.zeros((2 * p_dev, win), F32)
    for p in range(p_dev):
        off = off_ref[p]
        shift = jnp.where(off == 0, 0, raw_len - off)
        turned = pltpu.roll(raw, shift, 1)[:, :win]
        cut = jnp.where(row % p_dev == p, turned, cut)
    win_ref[me_p, me_t] = cut.astype(BF16)
    all_meta_ref[me_p, me_t] = meta_ref[...]
    pl.semaphore_wait(barrier, n_pulse - 1 + half - 1 + 1)

    def copies(pp, tt, send, recv, slot, target):
        return [
            pltpu.make_async_remote_copy(
                src_ref=ref.at[pp, tt],
                dst_ref=ref.at[pp, tt],
                send_sem=send.at[(a,) + slot],
                recv_sem=recv.at[(a,) + slot],
                device_id=target,
                device_id_type=MESH,
            )
            for a, ref in enumerate((win_ref, all_meta_ref))
        ]

    started = []

    def send(pp, tt, s, r, slot, target):
        for c in copies(pp, tt, s, r, slot, target):
            c.start()
            started.append(c)

    def arrive(pp, tt, s, r, slot, target):
        for c in copies(pp, tt, s, r, slot, target):
            c.wait_recv()

    for d in reversed(range(1, n_pulse)):
        send(me_p, me_t, z_send, z_recv, (d,), (pulse_peer(d), me_t))
    for dp in range(n_pulse):
        pp = lax.rem(me_p + n_pulse - dp, n_pulse)
        if dp:
            arrive(pp, me_t, z_send, z_recv, (dp,), (pulse_peer(dp), me_t))
        for dt in reversed(range(1, half)):
            send(pp, me_t, t_send, t_recv, (dp, dt), (me_p, tile_peer(dt)))
        send(pp, me_t, p_send, p_recv, (dp, 0), (me_p, partner))
    for dp in range(n_pulse):
        pp = lax.rem(me_p + n_pulse - dp, n_pulse)
        for dt in range(1, half):
            src = lax.rem(chip + half - dt, half) * 2 + core
            arrive(pp, src, t_send, t_recv, (dp, dt), (me_p, tile_peer(dt)))
            send(pp, src, p_send, p_recv, (dp, dt), (me_p, partner))
    for dp in range(n_pulse):
        pp = lax.rem(me_p + n_pulse - dp, n_pulse)
        for dt in range(half):
            src = lax.rem(chip + half - dt, half) * 2 + (1 - core)
            arrive(pp, src, p_send, p_recv, (dp, dt), (me_p, partner))
    for c in started:
        c.wait_send()


def gather(n_pulse, n_tile, range_off, raw, meta, win):
    rows = raw.shape[0]
    half = n_tile // 2
    sem = pltpu.SemaphoreType.DMA
    return pl.pallas_call(
        functools.partial(gather_kernel, n_pulse, n_tile),
        out_shape=(
            jax.ShapeDtypeStruct((n_pulse, n_tile, rows, win), BF16),
            jax.ShapeDtypeStruct((n_pulse, n_tile) + meta.shape, jnp.int32),
        ),
        in_specs=[
            pl.BlockSpec(memory_space=pltpu.SMEM),
            pl.BlockSpec(memory_space=pltpu.VMEM),
            pl.BlockSpec(memory_space=pltpu.VMEM),
        ],
        out_specs=[pl.BlockSpec(memory_space=pltpu.VMEM)] * 2,
        scratch_shapes=[
            sem((2, n_pulse)),
            sem((2, n_pulse)),
            sem((2, n_pulse, half)),
            sem((2, n_pulse, half)),
            sem((2, n_pulse, half)),
            sem((2, n_pulse, half)),
        ],
        compiler_params=pltpu.CompilerParams(collective_id=0, has_side_effects=True),
    )(range_off, raw, meta)


def spread(meta, field, rows8, n_rows):
    lane = lax.broadcasted_iota(jnp.int32, (meta.shape[1], n_rows), 0)
    col = lax.broadcasted_iota(jnp.int32, (meta.shape[1], n_rows), 1)
    pick = (lane == field * rows8 + col % rows8).astype(F32).astype(BF16)
    wide = jnp.dot(meta, pick, preferred_element_type=F32)
    owner = lax.broadcasted_iota(jnp.int32, wide.shape, 0)
    column = lax.broadcasted_iota(jnp.int32, wide.shape, 1)
    return jnp.sum(jnp.where(owner == column // rows8, wide, 0.0), axis=0, keepdims=True)


def thirds(x):
    a = x.astype(BF16)
    rest = x - a.astype(F32)
    b = rest.astype(BF16)
    return [a, b, (rest - b.astype(F32)).astype(BF16)]


def swap_parts(v, part1, p_dev):
    n = v.shape[-1]
    return jnp.where(part1, pltpu.roll(v, p_dev, 1), pltpu.roll(v, n - p_dev, 1))


def compress_kernel(
    steps, p_dev, idx_ref, meta_ref, win_ref, filt_ref,
    bands_ref, g_ref, vec_ref, x_ref, prof_ref, cut_ref,
):
    i = pl.program_id(0)
    n_rows, win = x_ref.shape[1:]
    rows8 = 2 * p_dev
    n_dev = n_rows // rows8
    chunk = filt_ref.shape[2]
    band = bands_ref.shape[1]
    pieces = band // LANES

    @pl.when(i == 0)
    def _():
        x = win_ref[...].astype(F32)
        r = lax.broadcasted_iota(jnp.int32, x.shape, 1)
        y = jnp.where(r < p_dev, -1.0, 1.0) * pltpu.roll(x, p_dev, 1)
        x_ref[0] = x.reshape(n_rows, win).astype(BF16)
        x_ref[1] = y.reshape(n_rows, win).astype(BF16)

    acc = jnp.dot(x_ref[0], filt_ref[0], preferred_element_type=F32) + jnp.dot(
        x_ref[1], filt_ref[1], preferred_element_type=F32
    )
    acc = acc.astype(BF16).astype(F32)
    stride = prof_ref.shape[0] // n_rows
    for c in range(chunk // LANES):
        prof_ref[pl.ds(i * (chunk // LANES) + c, n_rows, stride=stride), :] = acc[
            :, c * LANES : (c + 1) * LANES
        ]

    @pl.when(i == pl.num_programs(0) - 1)
    def _():
        tile = lax.axis_index("tile")
        lane = lax.broadcasted_iota(jnp.int32, (pieces, LANES), 1)

        def cut_owner(d, carry):
            for p in range(p_dev):
                start = idx_ref[d, 4 * rows8 + tile * p_dev + p]
                for b in range(2):
                    s = start + b
                    q = s // LANES
                    r = s % LANES
                    turn = jnp.where(r == 0, 0, LANES - r)
                    for part in range(2):
                        row = d * rows8 + part * p_dev + p
                        low = prof_ref[pl.ds(row * stride + q, pieces), :]
                        high = prof_ref[pl.ds(row * stride + q + 1, pieces), :]
                        cut_ref[pl.ds((b * n_rows + row) * pieces, pieces), :] = jnp.where(
                            lane < LANES - r, pltpu.roll(low, turn, 1), pltpu.roll(high, turn, 1)
                        )
            return carry

        lax.fori_loop(0, n_dev, cut_owner, 0)
        for c in range(pieces):
            bands_ref[:, c * LANES : (c + 1) * LANES] = cut_ref[
                pl.ds(c, 2 * n_rows, stride=pieces), :
            ].astype(BF16)

        meta = meta_ref[...].astype(F32).astype(BF16)
        blk = spread(meta, 0, rows8, n_rows)
        fine = spread(meta, 1, rows8, n_rows) * (1.0 / 16.0)
        dop = spread(meta, 2, rows8, n_rows) + DOP_SPLIT * spread(meta, 3, rows8, n_rows)
        sel = lax.broadcasted_iota(jnp.int32, (2 * steps, n_rows), 0)
        col = lax.broadcasted_iota(jnp.int32, (2 * steps, n_rows), 1)
        mine = ((sel // 2).astype(F32) == blk) & (sel % 2 == (col % rows8) // p_dev)
        zero = jnp.zeros((2 * steps, n_rows), F32)
        p_left = jnp.concatenate([jnp.where(mine, 1.0 - fine, zero), jnp.where(mine, fine, zero)], 1)
        q_left = jnp.concatenate([jnp.where(mine, -1.0, zero), jnp.where(mine, 1.0, zero)], 1)
        left = jnp.concatenate([p_left, q_left], 0).astype(BF16)
        pq = jnp.dot(left, bands_ref[...], preferred_element_type=F32)
        p_sum = pq[: 2 * steps]
        q_sum = pq[2 * steps :]
        x = 4.0 * p_sum + 1.5 * q_sum
        y = 1.5 * p_sum + 0.875 * q_sum
        xs = jnp.concatenate(thirds(x) + thirds(y), 0)
        d6 = lax.dot_general(
            xs, bands_ref[...], (((1,), (1,)), ((), ())), preferred_element_type=F32
        )
        k = 2 * steps
        dx = d6[2 * k : 3 * k] + d6[k : 2 * k] + d6[:k]
        dy = d6[5 * k : 6 * k] + d6[4 * k : 5 * k] + d6[3 * k : 4 * k]
        h = ((1.0 - fine) * dx[:, :n_rows] - dy[:, :n_rows]) + (
            fine * dx[:, n_rows:] + dy[:, n_rows:]
        )
        in_block = (sel // 2).astype(F32) == blk
        hr = jnp.sum(jnp.where(in_block & (sel % 2 == 0), h, 0.0), axis=0, keepdims=True)
        hi = jnp.sum(jnp.where(in_block & (sel % 2 == 1), h, 0.0), axis=0, keepdims=True)
        both = jnp.concatenate([hr, hi, jnp.zeros((6, n_rows), F32)], 0)
        part1 = (lax.broadcasted_iota(jnp.int32, (8, n_rows), 1) % rows8) >= p_dev
        other = swap_parts(both, part1, p_dev)
        hr, hi, hr_o, hi_o = both[0:1], both[1:2], other[0:1], other[1:2]
        one = part1[0:1]
        g_ref[0:1] = jnp.where(one, hr_o + hi, hr + hi_o)
        g_ref[1:2] = jnp.where(one, hr - hi_o, hr_o - hi)
        vec_ref[...] = jnp.concatenate([fine, dop, jnp.zeros((6, n_rows), F32)], 0)


def compress_all(steps, p_dev, meta, windows, filt, band):
    n_dev, rows8, win = windows.shape
    n_rows = n_dev * rows8
    ups = filt.shape[2]
    chunk = 2 * LANES
    chunks = ups // LANES
    pieces = band // LANES
    grid_spec = pltpu.PrefetchScalarGridSpec(
        num_scalar_prefetch=1,
        grid=(ups // chunk,),
        in_specs=[
            pl.BlockSpec(meta.shape, lambda i, s: (0, 0)),
            pl.BlockSpec(windows.shape, lambda i, s: (0, 0, 0)),
            pl.BlockSpec((2, win, chunk), lambda i, s: (0, 0, i)),
        ],
        out_specs=[
            pl.BlockSpec((2 * n_rows, band), lambda i, s: (0, 0)),
            pl.BlockSpec((2, n_rows), lambda i, s: (0, 0)),
            pl.BlockSpec((8, n_rows), lambda i, s: (0, 0)),
        ],
        scratch_shapes=[
            pltpu.VMEM((2, n_rows, win), BF16),
            pltpu.VMEM((n_rows * chunks + 8, LANES), F32),
            pltpu.VMEM((2 * n_rows * pieces, LANES), F32),
        ],
    )
    return pl.pallas_call(
        functools.partial(compress_kernel, steps, p_dev),
        out_shape=(
            jax.ShapeDtypeStruct((2 * n_rows, band), BF16),
            jax.ShapeDtypeStruct((2, n_rows), F32),
            jax.ShapeDtypeStruct((8, n_rows), F32),
        ),
        grid_spec=grid_spec,
        compiler_params=pltpu.CompilerParams(vmem_limit_bytes=VMEM_LIMIT),
    )(meta, meta, windows, filt)


def focus_kernel(n_pulse, n_tile, r_dev, p_dev, g_ref, vec_ref, left_ref, got_ref, send_sem, recv_sem):
    me_p = lax.axis_index("pulse")
    me_t = lax.axis_index("tile")
    n_rows = g_ref.shape[1]
    rows8 = 2 * p_dev
    total_rows = r_dev * n_pulse
    pulses = n_rows // 2
    barrier = pltpu.get_barrier_semaphore()

    def peer(d):
        return (me_p, lax.rem(me_t + d, n_tile))

    for d in range(1, n_tile):
        pl.semaphore_signal(barrier, 1, device_id=peer(d), device_id_type=MESH)
    pl.semaphore_wait(barrier, n_tile - 1)
    moves = [
        pltpu.make_async_remote_copy(
            src_ref=g_ref,
            dst_ref=got_ref.at[d],
            send_sem=send_sem.at[d],
            recv_sem=recv_sem.at[d],
            device_id=peer(d),
            device_id_type=MESH,
        )
        for d in range(1, n_tile)
    ]
    for move in moves:
        move.start()
    fine = vec_ref[0:1]
    dop = vec_ref[1:2].astype(jnp.int32)
    row = me_p * r_dev + lax.broadcasted_iota(jnp.int32, (r_dev, n_rows), 0)
    angle = 2.0 * jnp.pi * ((dop * row) & (total_rows - 1)).astype(F32) / total_rows
    norm = 1.0 / jnp.sqrt(F32(pulses))
    er = (jnp.cos(angle) * norm).astype(BF16).astype(F32)
    ei = (jnp.sin(angle) * norm).astype(BF16).astype(F32)
    total = g_ref[...]
    for d in range(1, n_tile):
        moves[d - 1].wait_recv()
        total = total + got_ref[d]
    g_re, g_im = total[0:1], total[1:2]
    scale = jnp.sqrt(g_re * g_re + g_im * g_im + 1.0)
    c_re = g_re / scale
    c_im = -g_im / scale
    one = (lax.broadcasted_iota(jnp.int32, (1, n_rows), 1) % rows8) >= p_dev
    alpha = jnp.where(one, -c_im, c_re)
    beta = jnp.where(one, c_re, c_im)
    w = (er * alpha - ei * beta, er * beta + ei * alpha)
    for z in range(2):
        here = pl.ds(z * r_dev, r_dev)
        left_ref[0, here, :n_rows] = (w[z] * (1.0 - fine)).astype(BF16)
        left_ref[0, here, n_rows:] = (w[z] * fine).astype(BF16)
        left_ref[1, here, :n_rows] = (w[z] * -fine).astype(BF16)
        left_ref[1, here, n_rows:] = (w[z] * (1.0 + fine)).astype(BF16)
    for move in moves:
        move.wait_send()


def focus(n_pulse, n_tile, r_dev, p_dev, g, vec):
    n_rows = g.shape[1]
    return pl.pallas_call(
        functools.partial(focus_kernel, n_pulse, n_tile, r_dev, p_dev),
        out_shape=jax.ShapeDtypeStruct((2, 2 * r_dev, 2 * n_rows), BF16),
        in_specs=[pl.BlockSpec(memory_space=pltpu.VMEM)] * 2,
        out_specs=pl.BlockSpec(memory_space=pltpu.VMEM),
        scratch_shapes=[
            pltpu.VMEM((n_tile,) + g.shape, F32),
            pltpu.SemaphoreType.DMA((n_tile,)),
            pltpu.SemaphoreType.DMA((n_tile,)),
        ],
        compiler_params=pltpu.CompilerParams(
            collective_id=1, has_side_effects=True, vmem_limit_bytes=VMEM_LIMIT
        ),
    )(g, vec)


def image_kernel(left_ref, bands_ref, out_ref, up_ref):
    r_dev = out_ref.shape[1]
    width = bands_ref.shape[1]
    out_chunk = 4 * LANES
    j = lax.broadcasted_iota(jnp.int32, up_ref.shape, 0)
    c = lax.broadcasted_iota(jnp.int32, up_ref.shape, 1)
    w = (c % 4).astype(F32) * 0.25
    up = jnp.where(j < LANES, 1.0 - w, w)
    up_ref[...] = jnp.where(j % LANES == c // 4, up, 0.0).astype(BF16)
    r0 = jnp.dot(left_ref[0], bands_ref[...], preferred_element_type=F32).astype(BF16)
    r1 = jnp.dot(left_ref[1], bands_ref[...], preferred_element_type=F32).astype(BF16)
    for s in range(width // LANES):
        cols = slice(s * LANES, (s + 1) * LANES)
        both = jnp.concatenate([r0[:, cols], r1[:, cols]], 1)
        res = jnp.dot(both, up_ref[...], preferred_element_type=F32).astype(BF16)
        for z in range(2):
            out_ref[z, :, s * out_chunk : (s + 1) * out_chunk] = res[z * r_dev : (z + 1) * r_dev]


def image(left, bands, r_dev):
    band = bands.shape[1]
    k = bands.shape[0]
    width = 2 * LANES
    return pl.pallas_call(
        image_kernel,
        grid=(band // width,),
        out_shape=jax.ShapeDtypeStruct((2, r_dev, 4 * band), BF16),
        in_specs=[
            pl.BlockSpec(left.shape, lambda i: (0, 0, 0)),
            pl.BlockSpec((k, width), lambda i: (0, i)),
        ],
        out_specs=pl.BlockSpec((2, r_dev, 4 * width), lambda i: (0, 0, i)),
        scratch_shapes=[pltpu.VMEM((2 * LANES, 4 * LANES), BF16)],
        compiler_params=pltpu.CompilerParams(vmem_limit_bytes=VMEM_LIMIT),
    )(left, bands)


BAND = 1024
R_DEV = 128


def shards(raw, filt, range_off, fine, dop, pulse_order, band_idx):
    n_pulse = lax.axis_size("pulse")
    n_tile = lax.axis_size("tile")
    p_dev = raw.shape[1]
    win = filt.shape[1]
    steps = pulse_order.shape[1]
    order = pulse_order[0]
    ids = jnp.arange(p_dev, dtype=jnp.int32)
    slot = jnp.arange(steps, dtype=jnp.int32)
    blk = jnp.sum(jnp.where(order[None, :] == ids[:, None], slot[None, :], 0), axis=1)
    meta = jnp.concatenate(
        [
            blk, blk, fine, fine,
            dop % DOP_SPLIT, dop % DOP_SPLIT, dop // DOP_SPLIT, dop // DOP_SPLIT,
            band_idx.reshape(-1),
        ]
    )
    meta = jnp.pad(meta, (0, -meta.shape[0] % LANES))[None]
    windows, all_meta = gather(
        n_pulse, n_tile, range_off, raw.reshape(2 * p_dev, -1), meta, win
    )
    n_dev = n_pulse * n_tile
    windows = windows.reshape(n_dev, 2 * p_dev, win)
    all_meta = all_meta.reshape(n_dev, -1)
    bands, g, vec = compress_all(steps, p_dev, all_meta, windows, filt, BAND)
    left = focus(n_pulse, n_tile, R_DEV, p_dev, g, vec)
    return image(left, bands, R_DEV)


def solution(mesh):
    return jax.shard_map(
        shards,
        mesh=mesh,
        in_specs=(
            P(None, ("pulse", "tile"), None),
            P(),
            P(("pulse", "tile")),
            P(("pulse", "tile")),
            P(("pulse", "tile")),
            P(("pulse", "tile"), None),
            P(None, ("pulse", "tile")),
        ),
        out_specs=P(None, "pulse", "tile"),
        check_vma=False,
    )
```

profile of v0, /device:TPU:0, one launch (start us, length us, event | category | flops | bytes accessed | tf_op | source)
XLA Modules:
  0.0 48.0 jit_solution(16769835529833594244)
XLA Ops:
  0.0 0.8 %select_reduce_fusion = s32[4]{0:T(128)S(1)} fusion(s32[4]{0:T(128)} %bitcast.8), kind=kLoop, calls=%fused_computation | loop fusion | flops 44 | bytes 32 | tf_op jit(solution)/shard_map/reduce_sum | solution.py:415
  0.8 0.7 %and_select_fusion = (s32[4]{0:T(128)S(1)}, s32[4]{0:T(128)S(1)}) fusion(s32[4]{0:T(128)} %param.11), kind=kLoop, calls=%fused_computation.2 | loop fusion | flops 76 | bytes 48 | tf_op jit(solution)/shard_map/jit(floor_divide)/jit(_where)/select_n | solution.py:419
  1.4 0.8 %copy.10 = s32[8,4]{1,0:T(8,128)S(1)} copy(s32[8,4]{0,1:T(4,128)} %param.13) | data formatting | bytes 256 | tf_op args[6]
  2.2 0.1 reshape.13
  2.3 0.8 %concatenate.3 = s32[64]{0:T(128)S(1)} concatenate(s32[4]{0:T(128)S(1)} %select_reduce_fusion, s32[4]{0:T(128)S(1)} %select_reduce_fusion, s32[4]{0:T(128)} %param.10, s32[4]{0:T(128)} %param.10, s32[4]{0:T(128)S(1)} %get-tuple-element.16, s32[4]{0:T(128)S(1)} %get-tuple-element.16, s32[4]{0:T(128)S(1)} %get-tuple-element.15, s32[4]{0:T(128)S(1)} %get-tuple-element.15, ...), dimensions={0} | concatenate | bytes 512 | tf_op jit(solution)/shard_map/concatenate | solution.py:416
  3.1 0.5 %pad_bitcast_fusion.meta_ref = s32[1,128]{1,0:T(1,128)} fusion(s32[64]{0:T(128)S(1)} %concatenate.3), kind=kLoop, calls=%fused_computation.7 | loop fusion | bytes 768 | tf_op jit(solution)/shard_map/broadcast_in_dim | solution.py:423
  3.6 1.4 %reshape.12.raw_ref = bf16[8,2048]{1,0:T(8,128)(2,1)} reshape(bf16[2,4,2048]{2,1,0:T(4,128)(2,1)} %param.7) | data formatting | bytes 65536 | tf_op jit(solution)/shard_map/reshape | solution.py:425
  5.0 16.8 %shard_map.73 = (bf16[4,8,8,1024]{3,2,1,0:T(8,128)(2,1)}, s32[4,8,1,128]{3,2,1,0:T(1,128)}) custom-call(s32[4]{0:T(128)} %off_ref.1, bf16[8,2048]{1,0:T(8,128)(2,1)} %reshape.12.raw_ref, s32[1,128]{1,0:T(1,128)} %pad_bitcast_fusion.meta_ref), custom_call_target="tpu_custom_call" | custom-call | tf_op jit(solution)/shard_map/pallas_call | solution.py:109
  21.8 15.1 %shard_map.74 = (bf16[512,1024]{1,0:T(8,128)(2,1)}, f32[2,256]{1,0:T(2,128)}, f32[8,256]{1,0:T(8,128)}) custom-call(s32[32,128]{1,0:T(8,128)} %bitcast.6, s32[32,128]{1,0:T(8,128)} %bitcast.7, bf16[32,8,1024]{2,1,0:T(8,128)(2,1)} %bitcast.5, bf16[2,1024,2048]{2,1,0:T(8,128)(2,1)} %filt_ref.1), custom_call_target="tpu_custom_call" | custom-call | tf_op jit(solution)/shard_map/pallas_call | solution.py:278
  36.9 6.3 %shard_map.75.left_ref = bf16[2,256,512]{2,1,0:T(8,128)(2,1)} custom-call(f32[2,256]{1,0:T(2,128)} %get-tuple-element.12.g_ref, f32[8,256]{1,0:T(8,128)} %get-tuple-element.13.vec_ref), custom_call_target="tpu_custom_call" | custom-call | tf_op jit(solution)/shard_map/pallas_call | solution.py:349
  43.3 4.7 %shard_map.76 = bf16[2,128,4096]{2,1,0:T(8,128)(2,1)} custom-call(bf16[2,256,512]{2,1,0:T(8,128)(2,1)} %shard_map.75.left_ref, bf16[512,1024]{1,0:T(8,128)(2,1)} %get-tuple-element.14.bands_ref), custom_call_target="tpu_custom_call" | custom-call | tf_op jit(solution)/shard_map/pallas_call | solution.py:388
where the time goes:
time: 48.6 us; the launch traced here: 48 us
  Pallas kernels  43 us (88%)
  local copies, waits for them, and re-layouts  3.54 us (7%)
  other arithmetic  1.44 us (3%)
    pallas_call x1, Pallas kernels, gather(): pl.pallas_call(functools.partial(gather_kernel, n_pulse, n_tile), out_sha...  16.8 us
    pallas_call x1, Pallas kernels, compress_all(): pl.pallas_call(functools.partial(compress_kernel, steps, p_dev), out_shap...  15.1 us
    pallas_call x1, Pallas kernels, focus(): pl.pallas_call(functools.partial(focus_kernel, n_pulse, n_tile, r_dev, p_...  6.34 us
    pallas_call x1, Pallas kernels, image(): pl.pallas_call(image_kernel, grid=(band // width,), out_shape=jax.ShapeDt...  4.74 us
    reshape x1, local copies, waits for them, and re-layouts, shards(): raw.reshape(2 * p_dev, -1)  1.38 us

commit v1 on v0

--- a/solution.py
+++ b/solution.py
@@ -16,7 +16,7 @@
 
 
 def gather_kernel(
-    n_pulse, n_tile, off_ref, raw_ref, meta_ref, win_ref, all_meta_ref,
+    n_pulse, n_tile, off_ref, fine_ref, dop_ref, order_ref, idx_ref, raw_ref, win_ref, all_meta_ref,
     z_send, z_recv, t_send, t_recv, p_send, p_recv,
 ):
     me_p = lax.axis_index("pulse")
@@ -25,8 +25,8 @@
     core = me_t % 2
     chip = me_t // 2
     partner = chip * 2 + (1 - core)
-    p_dev = raw_ref.shape[0] // 2
-    raw_len = raw_ref.shape[1]
+    p_dev = raw_ref.shape[1]
+    raw_len = raw_ref.shape[2]
     win = win_ref.shape[-1]
 
     def pulse_peer(d):
@@ -42,7 +42,7 @@
         pl.semaphore_signal(barrier, 1, device_id=(me_p, tile_peer(d)), device_id_type=MESH)
     pl.semaphore_signal(barrier, 1, device_id=(me_p, partner), device_id_type=MESH)
 
-    raw = raw_ref[...].astype(F32)
+    raw = jnp.concatenate([raw_ref[0].astype(F32), raw_ref[1].astype(F32)], 0)
     row = lax.broadcasted_iota(jnp.int32, (2 * p_dev, win), 0)
     cut = jnp.zeros((2 * p_dev, win), F32)
     for p in range(p_dev):
@@ -51,7 +51,18 @@
         turned = pltpu.roll(raw, shift, 1)[:, :win]
         cut = jnp.where(row % p_dev == p, turned, cut)
     win_ref[me_p, me_t] = cut.astype(BF16)
-    all_meta_ref[me_p, me_t] = meta_ref[...]
+    lane = lax.broadcasted_iota(jnp.int32, all_meta_ref.shape[2:], 1)
+    line = jnp.zeros(all_meta_ref.shape[2:], jnp.int32)
+    rows8 = 2 * p_dev
+    for p in range(p_dev):
+        pulse_lane = (lane < 4 * rows8) & (lane % p_dev == p)
+        line = jnp.where(pulse_lane & (lane // rows8 == 1), fine_ref[p], line)
+        line = jnp.where(pulse_lane & (lane // rows8 == 2), dop_ref[p] % DOP_SPLIT, line)
+        line = jnp.where(pulse_lane & (lane // rows8 == 3), dop_ref[p] // DOP_SPLIT, line)
+        line = jnp.where((lane < rows8) & (lane % p_dev == order_ref[0, p]), p, line)
+        for t in range(n_tile):
+            line = jnp.where(lane == 4 * rows8 + t * p_dev + p, idx_ref[t, p], line)
+    all_meta_ref[me_p, me_t] = line
     pl.semaphore_wait(barrier, n_pulse - 1 + half - 1 + 1)
 
     def copies(pp, tt, send, recv, slot, target):
@@ -102,21 +113,20 @@
         c.wait_send()
 
 
-def gather(n_pulse, n_tile, range_off, raw, meta, win):
-    rows = raw.shape[0]
+def gather(n_pulse, n_tile, range_off, fine, dop, order, idx, raw, win):
+    rows = 2 * raw.shape[1]
+    fields = 4 * rows + idx.size
+    width = fields + -fields % LANES
     half = n_tile // 2
     sem = pltpu.SemaphoreType.DMA
     return pl.pallas_call(
         functools.partial(gather_kernel, n_pulse, n_tile),
         out_shape=(
             jax.ShapeDtypeStruct((n_pulse, n_tile, rows, win), BF16),
-            jax.ShapeDtypeStruct((n_pulse, n_tile) + meta.shape, jnp.int32),
+            jax.ShapeDtypeStruct((n_pulse, n_tile, 1, width), jnp.int32),
         ),
-        in_specs=[
-            pl.BlockSpec(memory_space=pltpu.SMEM),
-            pl.BlockSpec(memory_space=pltpu.VMEM),
-            pl.BlockSpec(memory_space=pltpu.VMEM),
-        ],
+        in_specs=[pl.BlockSpec(memory_space=pltpu.SMEM)] * 5
+        + [pl.BlockSpec(memory_space=pltpu.VMEM)],
         out_specs=[pl.BlockSpec(memory_space=pltpu.VMEM)] * 2,
         scratch_shapes=[
             sem((2, n_pulse)),
@@ -127,7 +137,7 @@
             sem((2, n_pulse, half)),
         ],
         compiler_params=pltpu.CompilerParams(collective_id=0, has_side_effects=True),
-    )(range_off, raw, meta)
+    )(range_off, fine, dop, order, idx, raw)
 
 
 def spread(meta, field, rows8, n_rows):
@@ -204,7 +214,7 @@
                         )
             return carry
 
-        lax.fori_loop(0, n_dev, cut_owner, 0)
+        lax.fori_loop(0, n_dev, cut_owner, 0, unroll=4)
         for c in range(pieces):
             bands_ref[:, c * LANES : (c + 1) * LANES] = cut_ref[
                 pl.ds(c, 2 * n_rows, stride=pieces), :
@@ -409,20 +419,8 @@
     p_dev = raw.shape[1]
     win = filt.shape[1]
     steps = pulse_order.shape[1]
-    order = pulse_order[0]
-    ids = jnp.arange(p_dev, dtype=jnp.int32)
-    slot = jnp.arange(steps, dtype=jnp.int32)
-    blk = jnp.sum(jnp.where(order[None, :] == ids[:, None], slot[None, :], 0), axis=1)
-    meta = jnp.concatenate(
-        [
-            blk, blk, fine, fine,
-            dop % DOP_SPLIT, dop % DOP_SPLIT, dop // DOP_SPLIT, dop // DOP_SPLIT,
-            band_idx.reshape(-1),
-        ]
-    )
-    meta = jnp.pad(meta, (0, -meta.shape[0] % LANES))[None]
     windows, all_meta = gather(
-        n_pulse, n_tile, range_off, raw.reshape(2 * p_dev, -1), meta, win
+        n_pulse, n_tile, range_off, fine, dop, pulse_order, band_idx, raw, win
     )
     n_dev = n_pulse * n_tile
     windows = windows.reshape(n_dev, 2 * p_dev, win)

time: 48.6 us -> 43.5 us (0.90)
  local copies, waits for them, and re-layouts: 3.54 us -> 1.35 us
  other arithmetic: 1.44 us -> 0 us
  Pallas kernels: 43 us -> 41.6 us
    reshape x2 -> x0, local copies, waits for them, and re-layouts: 1.47 us -> none  [the longest x1 1.38 us: shards(): raw.reshape(2 * p_dev, -1)]
    pallas_call x1, Pallas kernels: 15.1 us -> 13.7 us  [compress_all(): pl.pallas_call(functools.partial(compress_kernel, steps, p_dev), out_shap...]
    concatenate x1 -> x0, local copies, waits for them, and re-layouts: 0.81 us -> none  [shards(): jnp.concatenate([blk, blk, fine, fine, dop % DOP_SPLIT, dop % DOP_SPLIT,...]
    reduce_sum x1 -> x0, other arithmetic: 0.77 us -> none  [shards(): jnp.sum(jnp.where(order[None, :] == ids[:, None], slot[None, :], 0), axis=1)]
    select_n x1 -> x0, other arithmetic: 0.67 us -> none  [shards(): dop // DOP_SPLIT]
    unnamed x1, local copies, waits for them, and re-layouts: 0.76 us -> 1.35 us
    broadcast_in_dim x1 -> x0, local copies, waits for them, and re-layouts: 0.51 us -> none  [shards(): meta = jnp.pad(meta, (0, -meta.shape[0] % LANES))[None]]
where the time goes in v1:
time: 43.5 us; the launch traced here: 42.9 us
  Pallas kernels  41.6 us (96%)
  local copies, waits for them, and re-layouts  1.35 us (3%)
    pallas_call x1, Pallas kernels, gather(): pl.pallas_call(functools.partial(gather_kernel, n_pulse, n_tile), out_sha...  16.8 us
    pallas_call x1, Pallas kernels, compress_all(): pl.pallas_call(functools.partial(compress_kernel, steps, p_dev), out_shap...  13.7 us
    pallas_call x1, Pallas kernels, focus(): pl.pallas_call(functools.partial(focus_kernel, n_pulse, n_tile, r_dev, p_...  6.33 us
    pallas_call x1, Pallas kernels, image(): pl.pallas_call(image_kernel, grid=(band // width,), out_shape=jax.ShapeDt...  4.73 us
    unnamed x1, local copies, waits for them, and re-layouts  1.35 us

profile of v1, /device:TPU:0, one launch (start us, length us, event | category | flops | bytes accessed | tf_op | source)
XLA Modules:
  0.0 42.9 jit_solution(17494664231268370173)
XLA Ops:
  0.0 1.3 %copy.8.idx_ref = s32[8,4]{1,0:T(8,128)} copy(s32[8,4]{0,1:T(4,128)} %param.13) | data formatting | bytes 256 | tf_op args[6]
  1.3 16.8 %shard_map.73 = (bf16[4,8,8,1024]{3,2,1,0:T(8,128)(2,1)}, s32[4,8,1,128]{3,2,1,0:T(1,128)}) custom-call(s32[4]{0:T(128)} %off_ref.1, s32[4]{0:T(128)} %fine_ref.1, s32[4]{0:T(128)} %dop_ref.1, s32[1,4]{1,0:T(1,128)} %order_ref.1, s32[8,4]{1,0:T(8,128)} %copy.8.idx_ref, bf16[2,4,2048]{2,1,0:T(4,128)(2,1)} %raw_ref.1), custom_call_target="tpu_custom_call" | custom-call | tf_op jit(solution)/shard_map/pallas_call | solution.py:122
  18.2 13.7 %shard_map.74 = (bf16[512,1024]{1,0:T(8,128)(2,1)}, f32[2,256]{1,0:T(2,128)}, f32[8,256]{1,0:T(8,128)}) custom-call(s32[32,128]{1,0:T(8,128)} %bitcast.3, s32[32,128]{1,0:T(8,128)} %bitcast.4, bf16[32,8,1024]{2,1,0:T(8,128)(2,1)} %bitcast.2, bf16[2,1024,2048]{2,1,0:T(8,128)(2,1)} %filt_ref.1), custom_call_target="tpu_custom_call" | custom-call | tf_op jit(solution)/shard_map/pallas_call | solution.py:288
  31.9 6.3 %shard_map.75.left_ref = bf16[2,256,512]{2,1,0:T(8,128)(2,1)} custom-call(f32[2,256]{1,0:T(2,128)} %get-tuple-element.12.g_ref, f32[8,256]{1,0:T(8,128)} %get-tuple-element.13.vec_ref), custom_call_target="tpu_custom_call" | custom-call | tf_op jit(solution)/shard_map/pallas_call | solution.py:359
  38.2 4.7 %shard_map.76 = bf16[2,128,4096]{2,1,0:T(8,128)(2,1)} custom-call(bf16[2,256,512]{2,1,0:T(8,128)(2,1)} %shard_map.75.left_ref, bf16[512,1024]{1,0:T(8,128)(2,1)} %get-tuple-element.14.bands_ref), custom_call_target="tpu_custom_call" | custom-call | tf_op jit(solution)/shard_map/pallas_call | solution.py:398
